TPU v7x, 32 devices: a whole 2x2x4 slice. The times are simulated.
32 devices in a mesh: seq: 16 (over z, x, core), tp: 2 (over y).
Axes of the slice: x: 2, y: 2, z: 4, core: 2. Of those that a mesh axis runs over, the one named last changes fastest.
Arguments:
- mixer_input: bfloat16 [8192, 3072], P('seq', 'tp'), may hold values from -6 to 6
- state_write: bfloat16 [8192, 128], P('seq'), may hold values from -2 to 2
- state_read: bfloat16 [8192, 128], P('seq'), may hold values from -2 to 2
- step_size: float32 [8192, 48], P('seq', 'tp'), may hold values from 0.05 to 0.5
- log_decay: float32 [8192, 48], P('seq', 'tp'), may hold values from -1.8 to 0, as said below
- skip_gain: float32 [48], P('tp'), may hold values from 0.5 to 2
- head_gain: float32 [3072], P('tp'), may hold values from 0.25 to 1.75
- mixer_out: bfloat16 [3072, 3072], P('tp'), may hold values from -0.109375 to 0.109375
- residual: bfloat16 [8192, 3072], P('seq', 'tp'), may hold values from -6 to 6
- attn_gain: float32 [3072], replicated, may hold values from 0.25 to 1.75
- qkv_weight: bfloat16 [3072, 3, 1536], P(None, None, 'tp'), may hold values from -2 to 2
Outputs:
- stream: bfloat16 [8192, 3072], P('seq', 'tp')
- attended: bfloat16 [8192, 1536], P('seq', 'tp')
Inputs may be any that keep to these rules, and one draw needn't show every extreme that they name: `log_decay`: negative everywhere.
All inputs are finite; a program needn't handle non-finite values.
Results may differ from a plain program's by a relative error of at most 0.03.
Values may be sent and summed in bfloat16 or wider, within the bound.
No kernel may reach another device: no remote copies, remote signals or barrier semaphores. Data moves between devices by JAX's collectives and lax.ppermute only.
A program may use at most 192 MiB of HBM per device.

v0:
```python
import jax
import jax.numpy as jnp
from jax import lax
from jax.sharding import PartitionSpec as P

AHD = 96
WINDOW = 2048


EPSILON = 1e-05


def prefix(x, axis, join, neutral):
    place = lax.axis_index(axis)
    gathered = jax.tree.map(
        lambda a, kind: lax.all_gather(a.astype(kind), axis),
        x,
        jax.tree.map(lambda a: jnp.bfloat16 if a.dtype == jnp.float32 else a.dtype, x),
    )
    state = jax.tree.map(lambda a, e: jnp.zeros_like(a) + jnp.asarray(e, a.dtype), x, neutral)

    def one(lap, state):
        return join(
            state,
            jax.tree.map(
                lambda a, own: lax.dynamic_index_in_dim(a, lap, 0, False).astype(own.dtype),
                gathered,
                x,
            ),
        )

    return lax.fori_loop(0, place, one, state)


def shifted(x, axis, by):
    size = lax.axis_size(axis)
    pairs = [(i, i + by) for i in range(size) if 0 <= i + by < size]
    return lax.ppermute(x, axis, pairs)


def span_terms(inputs, write_rows, read_rows, step_rows, decays, skip_gain):
    length, head_count = step_rows.shape
    head_dim = inputs.shape[1] // head_count
    cumulative = jnp.cumsum(decays, axis=0)
    totals = cumulative[-1]
    values = inputs.astype(jnp.float32).reshape(length, head_count, head_dim)
    scaled = (step_rows[:, :, None] * values).astype(jnp.bfloat16)
    intersection = jnp.dot(read_rows, write_rows.T, preferred_element_type=jnp.float32)
    sequence_place = jnp.arange(length)
    causal = sequence_place[:, None] >= sequence_place[None, :]
    log_gaps = cumulative.T[:, :, None] - cumulative.T[:, None, :]
    mixing = (
        jnp.where(causal, jnp.exp(jnp.where(causal, log_gaps, 0.0)), 0.0) * intersection
    ).astype(jnp.bfloat16)
    inner_part = jnp.einsum("hts,shp->thp", mixing, scaled, preferred_element_type=jnp.float32)
    local_part = inner_part + skip_gain[None, :, None] * values
    written = jnp.exp(totals[None, :] - cumulative)[:, :, None] * scaled.astype(jnp.float32)
    state_term = jnp.einsum(
        "shp,sn->hpn", written, write_rows.astype(jnp.float32), precision=lax.Precision.HIGHEST
    )
    return (local_part, state_term, totals, cumulative)


def join_states(earlier_pair, later_pair):
    return (
        earlier_pair[0] * later_pair[0],
        later_pair[0][:, None, None] * earlier_pair[1] + later_pair[1],
    )


def fold_spans(running, span_piece):
    state_term, totals = span_piece
    decay_run, state_run = running
    factor = jnp.exp(totals)
    return (
        (decay_run * factor, factor[:, None, None] * state_run + state_term),
        (decay_run, state_run),
    )


def on_device(
    mixer_input,
    state_write,
    state_read,
    step_size,
    log_decay,
    skip_gain,
    head_gain,
    mixer_out,
    residual,
    attn_gain,
    qkv_weight,
):
    tokens_dev = mixer_input.shape[0]
    head_count = step_size.shape[1]
    channels = mixer_input.shape[1]
    head_dim = channels // head_count
    span_len = min(tokens_dev, 256)
    span_count = tokens_dev // span_len

    def blocked(tensor):
        return tensor.reshape((span_count, span_len) + tensor.shape[1:])

    local_part, state_terms, totals, cumulative = jax.vmap(
        span_terms, in_axes=(0, 0, 0, 0, 0, None)
    )(
        blocked(mixer_input),
        blocked(state_write),
        blocked(state_read),
        blocked(step_size),
        blocked(log_decay),
        skip_gain,
    )
    identity_pair = (
        jnp.ones((head_count,), jnp.float32),
        jnp.zeros((head_count, head_dim, state_write.shape[1]), jnp.float32),
    )
    device_pair, before = lax.scan(fold_spans, identity_pair, (state_terms, totals))
    carry_in = prefix(device_pair, "seq", join_states, identity_pair)
    entering = before[0][:, :, None, None] * carry_in[1][None] + before[1]
    from_before = jnp.exp(cumulative)[..., None] * jnp.einsum(
        "ctn,chpn->cthp",
        blocked(state_read).astype(jnp.float32),
        entering,
        precision=lax.Precision.HIGHEST,
    )
    head_outputs = (local_part + from_before).reshape(tokens_dev, head_count, head_dim)
    inverse_rms = lax.rsqrt(jnp.mean(head_outputs * head_outputs, axis=2, keepdims=True) + EPSILON)
    normed = ((head_outputs * inverse_rms).reshape(tokens_dev, channels) * head_gain).astype(
        jnp.bfloat16
    )
    partial_value = jnp.dot(normed, mixer_out, preferred_element_type=jnp.float32)
    model_width = partial_value.shape[1]
    half_width = residual.shape[1]
    own_sum = lax.psum_scatter(
        partial_value.astype(jnp.bfloat16), "tp", scatter_dimension=1, tiled=True
    ).astype(jnp.float32)
    stream = (residual.astype(jnp.float32) + own_sum).astype(jnp.bfloat16)
    stream_wide = stream.astype(jnp.float32)
    squares = lax.psum(jnp.sum(stream_wide * stream_wide, axis=1), "tp")
    gain_half = lax.dynamic_slice_in_dim(
        attn_gain, lax.axis_index("tp") * half_width, half_width, 0
    )
    normed_half = (
        stream_wide * lax.rsqrt(squares / model_width + EPSILON)[:, None] * gain_half
    ).astype(jnp.bfloat16)
    normed_stream = lax.all_gather(normed_half, "tp", axis=1, tiled=True)
    projected = jnp.dot(
        normed_stream, qkv_weight.reshape(model_width, -1), preferred_element_type=jnp.float32
    ).astype(jnp.bfloat16)
    embed_dev = qkv_weight.shape[2]
    query_all = projected[:, :embed_dev]
    key_value = projected[:, embed_dev:]
    reach_blocks = WINDOW // tokens_dev
    earlier = jnp.concatenate(
        [shifted(key_value, "seq", offset) for offset in range(reach_blocks, 0, -1)], axis=0
    )
    context = jnp.concatenate([earlier, key_value], axis=0)
    attn_heads = embed_dev // AHD
    first_valid = WINDOW - lax.axis_index("seq") * tokens_dev
    query_block = min(tokens_dev, 512)
    queries = query_all.reshape(query_block, attn_heads, AHD)
    key_part = context[:, :embed_dev].reshape(-1, attn_heads, AHD)
    value_part = context[:, embed_dev:].reshape(-1, attn_heads, AHD)
    scores = jnp.einsum(
        "thd,rhd->htr", queries, key_part, preferred_element_type=jnp.float32
    ) * AHD ** (-0.5)
    query_pos = 0 + jnp.arange(query_block)
    key_pos = 0 + jnp.arange(context.shape[0])
    allowed = (
        (key_pos[None, :] > query_pos[:, None])
        & (key_pos[None, :] <= query_pos[:, None] + WINDOW)
        & (key_pos[None, :] >= first_valid)
    )
    masked = jnp.where(allowed[None], scores, -jnp.inf)
    peak = jnp.max(masked, axis=2, keepdims=True)
    raised = jnp.exp(masked - peak)
    weights = (raised / jnp.sum(raised, axis=2, keepdims=True)).astype(jnp.bfloat16)
    result = jnp.einsum("htr,rhd->thd", weights, value_part, preferred_element_type=jnp.float32)
    pieces = result.astype(jnp.bfloat16).reshape(query_block, embed_dev)
    return (stream, pieces)


def solution(mesh):
    placed = (
        P("seq", "tp"),
        P("seq", None),
        P("seq", None),
        P("seq", "tp"),
        P("seq", "tp"),
        P("tp"),
        P("tp"),
        P("tp", None),
        P("seq", "tp"),
        P(),
        P(None, None, "tp"),
    )
    return jax.shard_map(
        on_device,
        mesh=mesh,
        in_specs=placed,
        out_specs=(P("seq", "tp"), P("seq", "tp")),
        check_vma=False,
    )
```

profile of v0, /device:TPU:8, one launch (start us, length us, event | category | flops | bytes accessed | tf_op | source)
XLA Modules:
  0.0 423.0 jit_solution(155483758016515651)
XLA Ops:
  10.6 5.2 %reshape.195 = f32[2,256,24,64]{3,2,1,0:T(8,128)} reshape(bf16[512,1536]{1,0:T(8,128)(2,1)} %param.15) | data formatting | bytes 4718592 | tf_op jit(solution)/shard_map/vmap()/convert_element_type | solution.py:46
  15.7 6.2 %copy.81 = f32[2,256,24,64]{1,3,2,0:T(8,128)} copy(f32[2,256,24,64]{3,2,1,0:T(8,128)} %reshape.195) | data formatting | bytes 6291456 | tf_op jit(solution)/shard_map/vmap()/convert_element_type | solution.py:46
  21.9 3.6 fusion.24
  30.3 25.8 %all-reduce = bf16[384]{0:T(512)(128)(2,1)S(1)} all-reduce(bf16[384]{0:T(512)(128)(2,1)S(1)} %dynamic-update-slice), channel_id=2, replica_groups=mesh['seq'=16,'tp'=2] {'seq'}, use_global_device_ids=true, to_apply=%add | all-reduce | flops 384 | bytes 1536
  56.4 35.1 %all-gather.7.cloned.1.call-done = bf16[384,64,128]{2,1,0:T(8,128)(2,1)} async-done(((bf16[24,64,128]{2,1,0:T(8,128)(2,1)}), bf16[384,64,128]{2,1,0:T(8,128)(2,1)}) %all-gather.7.cloned.1.call-update) | async-done | bytes 6291472 | tf_op jit(solution)/shard_map/all_gather | solution.py:16
  91.6 5.3 %while.29 = (s32[]{:T(128)}, f32[24,64,128]{2,1,0:T(8,128)S(1)}, s32[]{:T(128)}, bf16[16,24]{1,0:T(8,128)(2,1)S(1)}, bf16[16,24,64,128]{3,2,1,0:T(8,128)(2,1)}, /*index=5*/s32[]{:T(128)}, s32[]{:T(128)}, s32[]{:T(128)}) while((s32[]{:T(128)}, f32[24,64,128]{2,1,0:T(8,128)S(1)}, s32[]{:T(128)}, bf16[16,24]{1,0:T(8,128)(2,1)S(1)}, ...), condition=%wide.region_5.6_spmd, body=%wide.region_4.5_spmd.sunk | while | flops 589853 | bytes 1966455 | solution.py:32
  98.8 4.0 multiply_reduce_fusion
  107.6 6.6 %convolution_convert_fusion.1 = bf16[512,3072]{1,0:T(8,128)(2,1)} fusion(bf16[512,1536]{0,1:T(8,128)(2,1)S(1)} %fusion.22, bf16[1536,3072]{1,0:T(8,128)(2,1)S(1)} %bitcast.123), kind=kOutput, calls=%fused_computation.31 | convolution fusion | flops 4833411072 | bytes 14155776 | tf_op jit(solution)/shard_map/dot_general | solution.py:132
  115.0 55.1 %reduce-scatter.2.cloned.1.call-done = bf16[512,1536]{1,0:T(8,128)(2,1)} async-done(((bf16[512,3072]{1,0:T(8,128)(2,1)}), bf16[512,1536]{1,0:T(8,128)(2,1)}) %reduce-scatter.2.cloned.1.call-update) | async-done | bytes 1572880 | tf_op jit(solution)/shard_map/reduce_scatter | solution.py:135
  172.2 5.2 %psum.7 = f32[512]{0:T(512)S(1)} all-reduce(f32[512]{0:T(512)S(1)} %get-tuple-element.153), channel_id=1, replica_groups=mesh['seq'=16,'tp'=2] {'tp'}, use_global_device_ids=true, to_apply=%region_9.10 | all-reduce | flops 512 | bytes 4096 | tf_op jit(solution)/shard_map/psum | solution.py:140
  179.0 18.8 %copy.88 = bf16[3072,3,768]{0,2,1:T(8,128)(2,1)} copy(bf16[3072,3,768]{2,0,1:T(8,128)(2,1)} %param.25) | data formatting | bytes 28311552 | tf_op args[10]
  197.9 26.2 %all-gather.5.cloned.1.call-done = bf16[512,3072]{1,0:T(8,128)(2,1)} async-done(((bf16[512,1536]{1,0:T(8,128)(2,1)}), bf16[512,3072]{1,0:T(8,128)(2,1)}) %all-gather.5.cloned.1.call-update) | async-done | bytes 3145744 | tf_op jit(solution)/shard_map/all_gather | solution.py:147
  224.1 12.5 %convolution_convert_fusion = bf16[512,2304]{1,0:T(8,128)(2,1)S(1)} fusion(bf16[512,3072]{1,0:T(8,128)(2,1)} %all-gather.5.cloned.1.call-done, bf16[3072,2304]{0,1:T(8,128)(2,1)} %bitcast.107), kind=kOutput, calls=%fused_computation.30 | convolution fusion | flops 7248936960 | bytes 19660800 | tf_op jit(solution)/shard_map/dot_general | solution.py:148
  237.8 3.4 collective-permute-start
  243.6 3.4 collective-permute-start.2
  253.4 23.9 %collective-permute-done = bf16[512,1536]{1,0:T(8,128)(2,1)} collective-permute-done((bf16[512,1536]{1,0:T(8,128)(2,1)}, bf16[512,1536]{1,0:T(8,128)(2,1)}, u32[]{:S(2)}, u32[]{:S(2)}) %collective-permute-start) | collective-permute-done | bytes 1572896 | tf_op jit(solution)/shard_map/ppermute | solution.py:38
  278.8 14.0 %collective-permute-done.1 = bf16[512,1536]{1,0:T(8,128)(2,1)} collective-permute-done((bf16[512,1536]{1,0:T(8,128)(2,1)}, bf16[512,1536]{1,0:T(8,128)(2,1)}, u32[]{:S(2)}, u32[]{:S(2)}) %collective-permute-start.1) | collective-permute-done | bytes 1572896 | tf_op jit(solution)/shard_map/ppermute | solution.py:38
  294.3 51.2 %collective-permute-done.2 = bf16[512,1536]{1,0:T(8,128)(2,1)} collective-permute-done((bf16[512,1536]{1,0:T(8,128)(2,1)}, bf16[512,1536]{1,0:T(8,128)(2,1)}, u32[]{:S(2)}, u32[]{:S(2)}) %collective-permute-start.2) | collective-permute-done | bytes 1572896 | tf_op jit(solution)/shard_map/ppermute | solution.py:38
  347.1 14.0 %collective-permute-done.3 = bf16[512,1536]{1,0:T(8,128)(2,1)} collective-permute-done((bf16[512,1536]{1,0:T(8,128)(2,1)}, bf16[512,1536]{1,0:T(8,128)(2,1)}, u32[]{:S(2)}, u32[]{:S(2)}) %collective-permute-start.3) | collective-permute-done | bytes 1572896 | tf_op jit(solution)/shard_map/ppermute | solution.py:38
  362.8 3.3 fusion.41
  366.1 6.2 %copy.91 = bf16[2560,768]{0,1:T(8,128)(2,1)} copy(bf16[2560,768]{1,0:T(8,128)(2,1)} %get-tuple-element.156) | data formatting | bytes 7864320 | tf_op jit(solution)/shard_map/slice | solution.py:163
  372.3 6.3 %copy.89 = bf16[2560,768]{0,1:T(8,128)(2,1)} copy(bf16[2560,768]{1,0:T(8,128)(2,1)} %get-tuple-element.157) | data formatting | bytes 7864320 | tf_op jit(solution)/shard_map/slice | solution.py:164
  378.7 20.4 %fusion.42 = (f32[8,512]{1,0:T(8,128)S(1)}, f32[8,512,2560]{2,1,0:T(8,128)}) fusion(pred[512,2560]{1,0:T(8,128)(4,1)S(1)} %copy-done.6, bf16[512,8,96]{0,2,1:T(8,128)(2,1)S(1)} %bitcast.112, bf16[2560,8,96]{0,2,1:T(8,128)(2,1)} %bitcast.110), kind=kOutput, calls=%fused_computation.81 | convolution fusion | flops 2055211520 | bytes 47988736 | tf_op jit(solution)/shard_map/sub | solution.py:177
  399.1 16.3 %fusion.31 = bf16[8,96,512]{2,1,0:T(8,128)(2,1)S(1)} fusion(bf16[2560,8,96]{0,2,1:T(8,128)(2,1)} %bitcast.111, f32[8,512,2560]{2,1,0:T(8,128)} %get-tuple-element.165, f32[8,512]{1,0:T(8,128)S(1)} %get-tuple-element.164), kind=kOutput, calls=%fused_computation.53 | convolution fusion | flops 2034630656 | bytes 46678016 | tf_op jit(solution)/shard_map/htr,rhd->thd/dot_general | solution.py:179
  (102 shorter events, 43.4 us)
Async XLA Ops:
  7.2 49.0 %copy-start = (bf16[512,128]{1,0:T(8,128)(2,1)S(1)}, bf16[512,128]{1,0:T(8,128)(2,1)}, u32[]{:S(2)}) copy-start(bf16[512,128]{1,0:T(8,128)(2,1)} %param.17) | copy-start | bytes 393220
  7.2 84.4 %all-gather.7.cloned.1.call-start = ((), (), s32[]{:S(2)}) async-start(), calls=%async_computation.3 | async-start | bytes 6684672 | tf_op jit(solution)/shard_map/all_gather | solution.py:16
  15.7 6.2 %copy-start.8 = (bf16[512,128]{1,0:T(8,128)(2,1)S(1)}, bf16[512,128]{1,0:T(8,128)(2,1)}, u32[]{:S(2)}) copy-start(bf16[512,128]{1,0:T(8,128)(2,1)} %param.16) | copy-start | bytes 393220
  25.5 3.2 copy-start.12
  28.7 141.5 %reduce-scatter.2.cloned.1.call-start = ((), (), s32[]{:S(2)}) async-start(), calls=%async_computation.1 | async-start | bytes 4718592 | tf_op jit(solution)/shard_map/reduce_scatter | solution.py:135
  91.6 5.3 %copy-start.5 = (f32[2,24,64,128]{3,2,1,0:T(8,128)S(1)}, f32[2,24,64,128]{3,2,1,0:T(8,128)}, u32[]{:S(2)}) copy-start(f32[2,24,64,128]{3,2,1,0:T(8,128)} %get-tuple-element.90) | copy-start | bytes 4718596
  96.9 1.9 copy-start.2
  97.0 1.9 copy-start.11
  102.9 3.6 slice-start
  102.9 3.6 slice-start.1
  105.4 0.7 copy-start.9
  105.4 2.2 slice-start.2
  114.2 0.7 copy-start.10
  114.3 55.9 %copy-start.4 = (bf16[512,1536]{1,0:T(8,128)(2,1)S(1)}, bf16[512,1536]{1,0:T(8,128)(2,1)}, u32[]{:S(2)}) copy-start(bf16[512,1536]{1,0:T(8,128)(2,1)} %param.23) | copy-start | bytes 4718596
  114.3 109.8 %all-gather.5.cloned.1.call-start = ((), (), s32[]{:S(2)}) async-start(), calls=%async_computation.2 | async-start | bytes 4718592 | tf_op jit(solution)/shard_map/all_gather | solution.py:147
  172.2 25.7 %copy-start.3 = (bf16[512,1536]{1,0:T(8,128)(2,1)}, bf16[512,1536]{1,0:T(8,128)(2,1)S(1)}, u32[]{:S(2)}) copy-start(bf16[512,1536]{1,0:T(8,128)(2,1)S(1)} %get-tuple-element.154) | copy-start | bytes 4718596
  237.8 39.5 %collective-permute-start = (bf16[512,1536]{1,0:T(8,128)(2,1)}, bf16[512,1536]{1,0:T(8,128)(2,1)}, u32[]{:S(2)}, u32[]{:S(2)}) collective-permute-start(bf16[512,1536]{1,0:T(8,128)(2,1)} %slice.31), channel_id=1, source_target_pairs={{0,8},{2,10},{4,12},{6,14},{8,16},{10,18},{12,20},{14,22},{16,24},... | collective-permute-start | bytes 4718600 | tf_op jit(solution)/shard_map/ppermute | solution.py:38
  241.2 51.6 %collective-permute-start.1 = (bf16[512,1536]{1,0:T(8,128)(2,1)}, bf16[512,1536]{1,0:T(8,128)(2,1)}, u32[]{:S(2)}, u32[]{:S(2)}) collective-permute-start(bf16[512,1536]{1,0:T(8,128)(2,1)} %slice.31), channel_id=1, source_target_pairs={{0,6},{2,8},{4,10},{6,12},{8,14},{10,16},{12,18},{14,20},{16,22},{... | collective-permute-start | bytes 4718600 | tf_op jit(solution)/shard_map/ppermute | solution.py:38
  243.6 102.0 %collective-permute-start.2 = (bf16[512,1536]{1,0:T(8,128)(2,1)}, bf16[512,1536]{1,0:T(8,128)(2,1)}, u32[]{:S(2)}, u32[]{:S(2)}) collective-permute-start(bf16[512,1536]{1,0:T(8,128)(2,1)} %slice.31), channel_id=1, source_target_pairs={{0,4},{2,6},{4,8},{6,10},{8,12},{10,14},{12,16},{14,18},{16,20},{1... | collective-permute-start | bytes 4718600 | tf_op jit(solution)/shard_map/ppermute | solution.py:38
  247.0 114.2 %collective-permute-start.3 = (bf16[512,1536]{1,0:T(8,128)(2,1)}, bf16[512,1536]{1,0:T(8,128)(2,1)}, u32[]{:S(2)}, u32[]{:S(2)}) collective-permute-start(bf16[512,1536]{1,0:T(8,128)(2,1)} %slice.31), channel_id=1, source_target_pairs={{0,2},{2,4},{4,6},{6,8},{8,10},{10,12},{12,14},{14,16},{16,18},{18... | collective-permute-start | bytes 4718600 | tf_op jit(solution)/shard_map/ppermute | solution.py:38
  372.3 6.4 %copy-start.6 = (pred[512,2560]{1,0:T(8,128)(4,1)S(1)}, pred[512,2560]{1,0:T(8,128)(4,1)}, u32[]{:S(2)}) copy-start(pred[512,2560]{1,0:T(8,128)(4,1)} %fusion.17) | copy-start | bytes 3932164
  372.3 6.4 %copy-start.7 = (bf16[512,768]{0,1:T(8,128)(2,1)S(1)}, bf16[512,768]{0,1:T(8,128)(2,1)}, u32[]{:S(2)}) copy-start(bf16[512,768]{0,1:T(8,128)(2,1)} %copy.90) | copy-start | bytes 2359300
  399.1 17.4 %copy-start.1 = (bf16[512,128]{1,0:T(8,128)(2,1)S(1)}, bf16[512,128]{1,0:T(8,128)(2,1)}, u32[]{:S(2)}) copy-start(bf16[512,128]{1,0:T(8,128)(2,1)} %param.17) | copy-start | bytes 393220
Sparse Core Ops, SparseCore 0:
  28.8 62.6 all-gather.6
  114.4 55.7 reduce-scatter.1
  179.1 44.8 all-gather.4
where the time goes:
time: 425 us; the launch traced here: 423 us
  waiting for transfers between devices  220 us (52%)
  matrix products  65 us (15%)
  local copies, waits for them, and re-layouts  64.3 us (15%)
  blocking collectives  30.9 us (7%)
  other arithmetic  15.9 us (4%)
  between operations  14.8 us (3%)
  starting transfers between devices  12 us (3%)
    ppermute x4, waiting for transfers between devices, shifted(): return lax.ppermute(x, axis, pairs)  103 us
    reduce_scatter x1, waiting for transfers between devices, on_device(): lax.psum_scatter(partial_value.astype(jnp.bfloat16), 'tp', scatter_dimens...  55.1 us
    all_gather x1, waiting for transfers between devices, prefix(): lax.all_gather(a.astype(kind), axis)  35.1 us
    unnamed x42, local copies, waits for them, and re-layouts  29.7 us
    all_gather x1, waiting for transfers between devices, on_device(): normed_stream = lax.all_gather(normed_half, 'tp', axis=1, tiled=True)  26.2 us
    unnamed x1, blocking collectives  25.8 us
    sub x1, matrix products, on_device(): raised = jnp.exp(masked - peak)  20.4 us
    dot_general x1, matrix products, on_device(): jnp.einsum('htr,rhd->thd', weights, value_part, preferred_element_type=jn...  16.3 us
  transfers between devices with their start and end apart: 7, of which 7 were waited for; matrix products, arithmetic and copies ran while one was open for 7% of the time, Pallas kernels for 0%

commit v1 on v0

v1 whole, which is shorter than its diff:
```python
import math

import jax
import jax.numpy as jnp
from jax import lax
from jax.experimental import pallas as pl
from jax.experimental.pallas import tpu as pltpu
from jax.sharding import PartitionSpec as P


AHD = 96
EPSILON = 1e-05
CHUNKS = (1, 1, 1, 1)
LOCAL = (3, 2, 1)


def attend(query, blocks, valid, head_dim):
    length, width = query.shape
    group = math.lcm(head_dim, 128)
    heads = group // head_dim
    groups = width // group
    pieces = [len(b) for b in blocks]
    flat = [p for b in blocks for p in b]
    n_full = len(blocks) - 2
    scale = head_dim ** (-0.5)

    def kernel(valid_ref, q_ref, *refs):
        k_refs, v_refs, at = [], [], 0
        for count in pieces:
            k_refs.append(refs[2 * at : 2 * (at + count) : 2])
            v_refs.append(refs[2 * at + 1 : 2 * (at + count) : 2])
            at += count
        o_ref, s_ref = refs[2 * at], refs[2 * at + 1]
        row = lax.broadcasted_iota(jnp.int32, (length, length), 0)
        col = lax.broadcasted_iota(jnp.int32, (length, length), 1)
        near = col <= row
        flags = [valid_ref[i] > 0 for i in range(1 + n_full)]
        far_bias = jnp.where(flags[0], 0.0, -jnp.inf)
        outs = {}
        for j in range(heads):
            lo = j * head_dim // 128 * 128
            hi = -(-(j + 1) * head_dim // 128) * 128
            lane = lo + lax.broadcasted_iota(jnp.int32, (length, hi - lo), 1)
            mine = (lane >= j * head_dim) & (lane < (j + 1) * head_dim)
            q = jnp.where(mine, q_ref[:, lo:hi], jnp.zeros((), q_ref.dtype))

            def load(refs):
                return jnp.concatenate([r[:, lo:hi] for r in refs], axis=0)

            def score(refs):
                return lax.dot_general(
                    q, load(refs), (((1,), (1,)), ((), ())), preferred_element_type=jnp.float32
                )

            def rowmax(s):
                return jnp.max(s, axis=1, keepdims=True)

            s = jnp.where(near, score(k_refs[-1]), score(k_refs[0]) + far_bias)
            s_ref[0] = s
            peak = rowmax(s)
            for i in range(n_full):
                s = score(k_refs[1 + i])
                s_ref[1 + i] = s
                peak = jnp.maximum(peak, jnp.where(flags[1 + i], rowmax(s), -jnp.inf))
            peak = peak * scale
            p = jnp.exp(s_ref[0] * scale - peak)
            total = jnp.sum(p, axis=1, keepdims=True)
            p = p.astype(jnp.bfloat16)
            zero = jnp.zeros_like(p)
            acc = jnp.dot(
                jnp.where(near, p, zero), load(v_refs[-1]), preferred_element_type=jnp.float32
            )
            acc += jnp.dot(
                jnp.where(near, zero, p), load(v_refs[0]), preferred_element_type=jnp.float32
            )
            for i in range(n_full):
                p = jnp.exp(s_ref[1 + i] * scale - jnp.where(flags[1 + i], peak, jnp.inf))
                total += jnp.sum(p, axis=1, keepdims=True)
                acc += jnp.dot(
                    p.astype(jnp.bfloat16), load(v_refs[1 + i]), preferred_element_type=jnp.float32
                )
            acc = acc * (1.0 / total)
            for t in range(lo, hi, 128):
                piece = jnp.where(mine[:, t - lo : t - lo + 128], acc[:, t - lo : t - lo + 128], 0.0)
                outs[t] = outs[t] + piece if t in outs else piece
        for t, piece in outs.items():
            o_ref[:, t : t + 128] = piece.astype(o_ref.dtype)

    specs = [
        pl.BlockSpec(memory_space=pltpu.SMEM),
        pl.BlockSpec((length, group), lambda g: (0, g)),
    ]
    args = [valid, query]
    for p in flat:
        specs.append(pl.BlockSpec((p.shape[0], group), lambda g: (0, g)))
        specs.append(pl.BlockSpec((p.shape[0], group), lambda g: (0, g + groups)))
        args += [p, p]
    keys = len(blocks) * length
    return pl.pallas_call(
        kernel,
        grid=(groups,),
        in_specs=specs,
        out_specs=pl.BlockSpec((length, group), lambda g: (0, g)),
        out_shape=jax.ShapeDtypeStruct((length, width), query.dtype),
        scratch_shapes=[pltpu.VMEM((1 + n_full, length, length), jnp.float32)],
        cost_estimate=pl.CostEstimate(
            flops=4 * length * keys * width,
            transcendentals=length * keys * width // head_dim,
            bytes_accessed=2 * (len(blocks) * 2 + 2) * length * width,
        ),
        compiler_params=pltpu.CompilerParams(vmem_limit_bytes=31 << 20),
        name="attend",
    )(*args)


def stream_and_project(own, got, residual, far_residual, side, gain, weight, at, buffers):
    rows, width = own.shape
    length, half = residual.shape
    parts, _, embed = weight.shape
    tile = embed // 2
    steps = embed // tile
    index = at // rows

    def kernel(side_ref, own_ref, got_ref, res_ref, far_ref, gain_ref, w_ref, *refs):
        stream_ref, n_ref, kv_ref, w_sum = refs[len(buffers) :]
        first = side_ref[0] == 0

        @pl.when(pl.program_id(0) == 0)
        def _():
            squares = jnp.zeros((rows, 1), jnp.float32)
            kept = []
            for h in range(2):
                lanes = slice(h * half, (h + 1) * half)
                base = jnp.where(first == (h == 0), res_ref[...], far_ref[...])
                wide = base.astype(jnp.float32) + (
                    own_ref[:, lanes].astype(jnp.float32) + got_ref[:, lanes].astype(jnp.float32)
                )
                stream = wide.astype(own_ref.dtype)
                kept.append(stream)
                wide = stream.astype(jnp.float32)
                w_sum[:, lanes] = wide
                squares += jnp.sum(wide * wide, axis=1, keepdims=True)
            stream_ref[...] = jnp.where(first, kept[0], kept[1])
            inverse = lax.rsqrt(squares / width + EPSILON)
            n_ref[...] = (w_sum[...] * inverse * gain_ref[...]).astype(n_ref.dtype)

        kv_ref[...] = jnp.dot(n_ref[...], w_ref[0], preferred_element_type=jnp.float32).astype(
            kv_ref.dtype
        )

    flat = lambda a: pl.BlockSpec(a.shape, lambda i: (0, 0))
    return pl.pallas_call(
        kernel,
        grid=((parts - 1) * steps,),
        in_specs=[
            pl.BlockSpec(memory_space=pltpu.SMEM),
            flat(own),
            flat(got),
            pl.BlockSpec((rows, half), lambda i: (index, 0)),
            pl.BlockSpec((rows, half), lambda i: (index, 0)),
            flat(gain),
            pl.BlockSpec((1, width, tile), lambda i: (1 + i // steps, 0, i % steps)),
        ]
        + [pl.BlockSpec(memory_space=pl.ANY)] * len(buffers),
        out_specs=[
            pl.BlockSpec((rows, half), lambda i: (index, 0)),
            pl.BlockSpec((rows, width), lambda i: (index, 0)),
            pl.BlockSpec((rows, tile), lambda i: (0, i)),
        ],
        out_shape=[
            jax.ShapeDtypeStruct((length, half), own.dtype),
            jax.ShapeDtypeStruct((length, width), own.dtype),
            pltpu.HBM((rows, (parts - 1) * embed), own.dtype),
        ],
        scratch_shapes=[pltpu.VMEM((rows, width), jnp.float32)],
        input_output_aliases={7 + i: i for i in range(len(buffers))},
        cost_estimate=pl.CostEstimate(
            flops=2 * rows * width * (parts - 1) * embed,
            transcendentals=rows,
            bytes_accessed=2 * width * (parts - 1) * embed,
        ),
        compiler_params=pltpu.CompilerParams(vmem_limit_bytes=17 << 20),
        name="stream_and_project",
    )(side, *held(own), got, *held(residual, far_residual, gain), weight, *buffers)


def project_queries(normed_stream, weight):
    length, width = normed_stream.shape
    embed = weight.shape[2]
    tile = embed // 3

    def kernel(n_ref, w_ref, q_ref):
        q_ref[...] = jnp.dot(n_ref[...], w_ref[0], preferred_element_type=jnp.float32).astype(
            q_ref.dtype
        )

    return pl.pallas_call(
        kernel,
        grid=(embed // tile,),
        in_specs=[
            pl.BlockSpec((length, width), lambda i: (0, 0)),
            pl.BlockSpec((1, width, tile), lambda i: (0, 0, i)),
        ],
        out_specs=pl.BlockSpec((length, tile), lambda i: (0, i)),
        out_shape=jax.ShapeDtypeStruct((length, embed), normed_stream.dtype),
        cost_estimate=pl.CostEstimate(
            flops=2 * length * width * embed,
            transcendentals=0,
            bytes_accessed=2 * width * (embed + length),
        ),
        compiler_params=pltpu.CompilerParams(vmem_limit_bytes=14 << 20),
        name="project_queries",
    )(normed_stream, weight)


def held(*arrays):
    return [pltpu.with_memory_space_constraint(a, pltpu.HBM) for a in arrays]


def log2(n):
    return n.bit_length() - 1


def expander(first, kind, group, head_dim, slots):
    row = lax.broadcasted_iota(jnp.int32, (128, group), 0)
    lane = lax.broadcasted_iota(jnp.int32, (128, group), 1)
    gap = row - (kind * 2 * slots + first) - lax.shift_right_logical(lane, log2(head_dim))
    return ((gap == 0) | (gap == slots)).astype(jnp.bfloat16)


def terms(a):
    high = a.astype(jnp.bfloat16).astype(jnp.float32)
    return [high, a - high]


def write_states(inputs, step_rows, decay_rows, write_rows, head_dim, slots, heads, spans):
    length, channels = inputs.shape
    head_count = step_rows.shape[0]
    size = write_rows.shape[1]
    span = length // spans
    group = heads * head_dim

    def kernel(x_ref, p_ref, d_ref, b_ref, o_ref, steps_ref, fades_ref, carries_ref, gaps_ref, rows_ref):
        i = pl.program_id(0)

        @pl.when(i == 0)
        def _():
            before = lax.broadcasted_iota(jnp.int32, (span, span), 0)
            after = lax.broadcasted_iota(jnp.int32, (span, span), 1)
            ones = (before <= after).astype(jnp.float32)
            start = jnp.zeros((head_count, 1), jnp.float32)
            grown, overall, ends = [], [], []
            for s in range(spans):
                part = jnp.dot(
                    d_ref[:, s * span : (s + 1) * span],
                    ones,
                    preferred_element_type=jnp.float32,
                    precision=lax.Precision.HIGHEST,
                )
                last = part[:, span - 1 :]
                grown.append(part)
                overall.append(part + start)
                ends.append(jnp.broadcast_to(last, (head_count, span)))
                start = start + last
            grown, overall, ends = (jnp.concatenate(a, axis=1) for a in (grown, overall, ends))
            rows_ref[...] = grown
            pad = jnp.zeros((slots - head_count, length), jnp.float32)

            def columns(parts):
                stacked = [a for part in parts for a in (part, pad)]
                rest = 128 - slots * len(parts)
                if rest:
                    stacked.append(jnp.zeros((rest, length), jnp.float32))
                return jnp.concatenate(stacked, axis=0).T

            step = p_ref[...]
            steps_ref[...] = columns(terms(step * jnp.exp(start - overall)) + terms(step)).astype(
                jnp.bfloat16
            )
            fades_ref[...] = columns(terms(jnp.exp(grown)) + terms(jnp.exp(ends - grown))).astype(
                jnp.bfloat16
            )
            carries_ref[...] = columns(terms(jnp.exp(overall))).astype(jnp.bfloat16)
            gaps_ref[...] = columns([grown])
            decay = jnp.broadcast_to(jnp.exp(start), (head_count, size))
            o_ref[channels:, :] = jnp.concatenate(terms(decay), axis=0).astype(jnp.bfloat16)

        spread = expander(i * heads, 0, group, head_dim, slots)
        weight = jnp.dot(steps_ref[...], spread, preferred_element_type=jnp.float32)
        u = (x_ref[...].astype(jnp.float32) * weight).astype(jnp.bfloat16)
        o_ref[pl.ds(pl.multiple_of(i * group, group), group), :] = lax.dot_general(
            u, b_ref[...], (((0,), (0,)), ((), ())), preferred_element_type=jnp.float32
        ).astype(o_ref.dtype)

    full = lambda a: pl.BlockSpec(a.shape, lambda i: (0, 0))
    shapes = [
        pltpu.HBM((channels + 2 * head_count, size), jnp.bfloat16),
        pltpu.HBM((length, 128), jnp.bfloat16),
        pltpu.HBM((length, 128), jnp.bfloat16),
        pltpu.HBM((length, 128), jnp.bfloat16),
        pltpu.HBM((length, 128), jnp.float32),
        pltpu.HBM((head_count, length), jnp.float32),
    ]
    return pl.pallas_call(
        kernel,
        grid=(channels // group,),
        in_specs=[
            pl.BlockSpec((length, group), lambda i: (0, i)),
            full(step_rows),
            full(decay_rows),
            full(write_rows),
        ],
        out_specs=[full(a) for a in shapes],
        out_shape=shapes,
        cost_estimate=pl.CostEstimate(
            flops=2 * length * channels * size,
            transcendentals=0,
            bytes_accessed=2 * (length + size) * channels,
        ),
        compiler_params=pltpu.CompilerParams(vmem_limit_bytes=14 << 20),
        name="write_states",
    )(*held(inputs, step_rows, decay_rows, write_rows))


def local_outputs(
    inputs, steps, fades, grown, rows, write_rows, read_rows, skip, head_dim, slots, heads, spans,
    offset, count, buffers,
):
    length, channels = inputs.shape
    span = length // spans
    wide = 2 * head_dim
    group = heads * head_dim

    def kernel(x_ref, p_ref, f_ref, t_ref, g_ref, b_ref, c_ref, k_ref, *refs):
        o_ref, i_ref = refs[len(buffers) :]
        first = (pl.program_id(0) + offset) * heads

        @pl.when(pl.program_id(0) == 0)
        def _():
            for s in range(spans):
                at = s * span
                inner = lax.dot_general(
                    c_ref[at : at + span, :],
                    b_ref[at : at + span, :],
                    (((1,), (1,)), ((), ())),
                    preferred_element_type=jnp.float32,
                )
                row = lax.broadcasted_iota(jnp.int32, (span, span), 0)
                col = lax.broadcasted_iota(jnp.int32, (span, span), 1)
                i_ref[s] = jnp.where(row >= col, inner, 0.0)

        columns = pltpu.roll(t_ref[...], lax.rem(t_ref.shape[1] - first, t_ref.shape[1]), 1)
        step = jnp.dot(
            p_ref[...],
            expander(first, 1, group, head_dim, slots),
            preferred_element_type=jnp.float32,
        )
        grow = jnp.dot(
            f_ref[...],
            expander(first, 0, group, head_dim, slots),
            preferred_element_type=jnp.float32,
        )
        fade = jnp.dot(
            f_ref[...],
            expander(first, 1, group, head_dim, slots),
            preferred_element_type=jnp.float32,
        )
        lane = lax.broadcasted_iota(jnp.int32, (span, wide), 1)
        for pair in range(heads // 2):
            at = slice(pair * wide, (pair + 1) * wide)
            state = None
            for s in range(spans):
                here = slice(s * span, (s + 1) * span)
                x = x_ref[here, at].astype(jnp.float32)
                u = (step[here, at] * x).astype(jnp.bfloat16)
                out = k_ref[:, at] * x
                for j in range(2):
                    head = 2 * pair + j
                    gap = columns[here, head : head + 1] - g_ref[0, head : head + 1, here]
                    mixing = (jnp.exp(jnp.minimum(gap, 0.0)) * i_ref[s]).astype(jnp.bfloat16)
                    mine = (lane >= head_dim) if j else (lane < head_dim)
                    out += jnp.dot(
                        mixing,
                        jnp.where(mine, u, jnp.zeros_like(u)),
                        preferred_element_type=jnp.float32,
                    )
                if s:
                    out += grow[here, at] * jnp.dot(
                        c_ref[here, :], state.astype(jnp.bfloat16), preferred_element_type=jnp.float32
                    )
                if s + 1 < spans:
                    weighted = (u.astype(jnp.float32) * fade[here, at]).astype(jnp.bfloat16)
                    fresh = lax.dot_general(
                        b_ref[here, :],
                        weighted,
                        (((0,), (0,)), ((), ())),
                        preferred_element_type=jnp.float32,
                    )
                    last = grow[(s + 1) * span - 1 : (s + 1) * span, at]
                    state = fresh if state is None else last * state + fresh
                o_ref[here, at] = out

    full = lambda a: pl.BlockSpec(a.shape, lambda i: (0,) * a.ndim)
    return pl.pallas_call(
        kernel,
        grid=(count,),
        in_specs=[
            pl.BlockSpec((length, group), lambda i: (0, i + offset)),
            full(steps),
            full(fades),
            full(grown),
            pl.BlockSpec((1, heads, length), lambda i: (i + offset, 0, 0)),
            full(write_rows),
            full(read_rows),
            pl.BlockSpec((1, group), lambda i: (0, i + offset)),
        ]
        + [pl.BlockSpec(memory_space=pl.ANY)] * len(buffers),
        out_specs=pl.BlockSpec((length, group), lambda i: (0, i + offset)),
        out_shape=pltpu.HBM((length, channels), jnp.float32),
        scratch_shapes=[pltpu.VMEM((spans, span, span), jnp.float32)],
        input_output_aliases={8: 0} if buffers else {},
        cost_estimate=pl.CostEstimate(
            flops=2 * length * count * group * span * 2,
            transcendentals=length * span * count * heads,
            bytes_accessed=6 * length * count * group,
        ),
        compiler_params=pltpu.CompilerParams(vmem_limit_bytes=14 << 20),
        name="local_outputs",
    )(*held(inputs, steps, fades, grown, rows, write_rows, read_rows, skip, *buffers))


def partial_outputs(
    local, packed, read_rows, entering, gain, weight, head_dim, slots, heads, at, sizes
):
    length, channels = local.shape
    width = weight.shape[1]
    group = heads * head_dim
    tile = width // 4
    here = slice(at, at + sum(sizes))

    def kernel(y_ref, p_ref, c_ref, s_ref, g_ref, w_ref, *refs):
        o_refs, a_ref = refs[:-1], refs[-1]
        i = pl.program_id(0)
        row = lax.broadcasted_iota(jnp.int32, (group, group), 0)
        col = lax.broadcasted_iota(jnp.int32, (group, group), 1)
        same = (lax.bitwise_xor(row, col) < head_dim).astype(jnp.bfloat16)
        carried = lax.dot_general(
            c_ref[here, :], s_ref[...], (((1,), (1,)), ((), ())), preferred_element_type=jnp.float32
        )
        spread = expander(i * heads, 0, group, head_dim, slots)
        factor = jnp.dot(p_ref[here, :], spread, preferred_element_type=jnp.float32)
        y = y_ref[here, :] + carried * factor
        square = y * y
        high = square.astype(jnp.bfloat16)
        low = (square - high.astype(jnp.float32)).astype(jnp.bfloat16)
        sums = jnp.dot(high, same, preferred_element_type=jnp.float32) + jnp.dot(
            low, same, preferred_element_type=jnp.float32
        )
        y = (y * lax.rsqrt(sums / head_dim + EPSILON) * g_ref[...]).astype(jnp.bfloat16)

        @pl.when(i == 0)
        def _():
            a_ref[...] = jnp.zeros_like(a_ref)

        for t in range(0, width, tile):
            a_ref[:, t : t + tile] += jnp.dot(
                y, w_ref[:, t : t + tile], preferred_element_type=jnp.float32
            )

        @pl.when(i + 1 == pl.num_programs(0))
        def _():
            top = 0
            for o_ref in o_refs:
                o_ref[...] = a_ref[top : top + o_ref.shape[0], :].astype(o_ref.dtype)
                top += o_ref.shape[0]

    rows = sum(sizes)
    return pl.pallas_call(
        kernel,
        grid=(channels // group,),
        in_specs=[
            pl.BlockSpec((length, group), lambda i: (0, i)),
            pl.BlockSpec(packed.shape, lambda i: (0, 0)),
            pl.BlockSpec(read_rows.shape, lambda i: (0, 0)),
            pl.BlockSpec((group, read_rows.shape[1]), lambda i: (i, 0)),
            pl.BlockSpec((1, group), lambda i: (0, i)),
            pl.BlockSpec((group, width), lambda i: (i, 0)),
        ],
        out_specs=[pl.BlockSpec((n, width), lambda i: (0, 0)) for n in sizes],
        out_shape=[pltpu.HBM((n, width), jnp.bfloat16) for n in sizes],
        scratch_shapes=[pltpu.VMEM((rows, width), jnp.float32)],
        cost_estimate=pl.CostEstimate(
            flops=2 * rows * channels * width,
            transcendentals=rows * channels,
            bytes_accessed=2 * width * channels,
        ),
        compiler_params=pltpu.CompilerParams(vmem_limit_bytes=23 << 20),
        name="partial_outputs",
    )(*held(local, packed, read_rows), entering, gain, weight)


def flip(x, bit):
    size = lax.axis_size("seq")
    return lax.ppermute(x, "seq", [(i, i ^ bit) for i in range(size)])


def shift(x, by):
    size = lax.axis_size("seq")
    return lax.ppermute(x, "seq", [(i, i + by) for i in range(size - by)])


def swap(x):
    return lax.ppermute(x, "tp", [(0, 1), (1, 0)])


def pack(state, decay):
    high = decay.astype(jnp.bfloat16)
    low = (decay - high.astype(jnp.float32)).astype(jnp.bfloat16)
    size = state.shape[2]
    return jnp.concatenate(
        [state.astype(jnp.bfloat16).reshape(-1, size), high.reshape(-1, size), low.reshape(-1, size)]
    )


def unpack(rows, heads):
    size = rows.shape[1]
    at = rows.shape[0] - 2 * heads
    state = rows[:at].astype(jnp.float32).reshape(heads, -1, size)
    tail = rows[at:].astype(jnp.float32)
    return state, (tail[:heads] + tail[heads:]).reshape(heads, 1, size)


def entering_state(rows, heads):
    place = lax.axis_index("seq")
    planes = lax.axis_size("seq") // 4
    core = place % 2
    side = place // 2 % 2
    half, quarter = heads // 2, heads // 4

    def part(pair, index, size):
        return tuple(lax.dynamic_slice_in_dim(a, index * size, size, 0) for a in pair)

    def ordered(mine, other, bit):
        first = jax.tree.map(lambda a, b: jnp.where(bit == 0, a, b), mine, other)
        second = jax.tree.map(lambda a, b: jnp.where(bit == 0, b, a), mine, other)
        return first, second

    def joined(first, second):
        return second[1] * first[0] + second[0], first[1] * second[1]

    mine = unpack(rows, heads)
    other = flip(rows, 1)
    other = unpack(other, heads)
    first, second = ordered(mine, other, core)
    chip = joined(part(first, core, half), part(second, core, half))
    chip_rows = pack(*chip)
    chip = unpack(chip_rows, half)
    other_chip = flip(chip_rows, 2)
    first_chip, second_chip = ordered(chip, unpack(other_chip, half), side)
    plane_rows = pack(*joined(part(first_chip, side, quarter), part(second_chip, side, quarter)))
    before = jnp.zeros((quarter,) + chip[0].shape[1:], jnp.float32)
    arrived = []
    for by in range(1, planes):
        arrived.append(shift(plane_rows, 4 * by))
    for state, decay in [unpack(a, quarter) for a in reversed(arrived)]:
        before = state + decay * before
    before = before.astype(jnp.bfloat16)

    def whole(own, bit, distance):
        got = flip(own, distance)
        return jnp.where(
            bit == 0, jnp.concatenate([own, got]), jnp.concatenate([got, own])
        ).astype(jnp.float32)

    before = whole(before, side, 2)
    before = jnp.where(side == 1, first_chip[1] * before + first_chip[0], before)
    before = whole(before.astype(jnp.bfloat16), core, 1)
    return jnp.where(core == 1, first[1] * before + first[0], before).astype(jnp.bfloat16)


def on_device(
    mixer_input, state_write, state_read, step_size, log_decay, skip_gain, head_gain,
    mixer_out, residual, attn_gain, qkv_weight,
):
    tokens, channels = mixer_input.shape
    head_count = step_size.shape[1]
    head_dim = channels // head_count
    span_len = min(tokens, 256)
    spans = tokens // span_len
    slots = 32
    heads = 4
    side = lax.axis_index("tp")
    far_residual = swap(residual)

    payload, steps, fades, carries, gaps, rows = write_states(
        mixer_input, step_size.T, log_decay.T, state_write, head_dim, slots, heads, spans
    )
    rows = rows.reshape(head_count // heads, heads, tokens)
    size = payload.shape[1]
    local, offset = [], 0
    for count in LOCAL:
        count = head_count // heads * count // sum(LOCAL)
        local = [
            local_outputs(
                mixer_input, steps, fades, gaps, rows, state_write, state_read,
                jnp.repeat(skip_gain, head_dim)[None], head_dim, slots, heads, spans,
                offset, count, local,
            )
        ]
        offset += count
    entering = entering_state(payload, head_count).reshape(channels, size)

    weight = jnp.transpose(qkv_weight, (1, 0, 2))
    place = lax.axis_index("seq")
    core = place % 2
    plane_side = place // 2 % 2
    sizes = [tokens * count // sum(CHUNKS) for count in CHUNKS]
    owns, done = [], 0
    for some in (sizes[:1], sizes[1:]):
        owns += partial_outputs(
            local[0], carries, state_read, entering, head_gain[None], mixer_out, head_dim,
            slots, heads, done, some,
        )
        done += sum(some)
    at, buffers, kept = 0, [], [[], [], [], [], []]
    for k, count in enumerate(CHUNKS):
        rows = tokens * count // sum(CHUNKS)
        own = owns[k]
        got = swap(own)
        *buffers, mine = stream_and_project(
            own, got, residual, far_residual, side[None], attn_gain[None], weight, at, buffers
        )
        far = shift(mine, 4)
        near = flip(jnp.where(core == 0, mine, far), 1)
        across = flip(jnp.where(plane_side == 0, mine, far), 2)
        corner = flip(across, 1)
        for held, piece in zip(kept, (far, near, across, corner, mine)):
            held.append(piece)
        at += rows
    streams, normed_stream = buffers
    queries = project_queries(normed_stream, weight)
    back = jnp.stack(
        [4 + 0 * core, jnp.where(core == 1, 1, 3), 2 + 0 * core, jnp.where(core == 1, 3, 1)]
    )
    valid = (place >= back).astype(jnp.int32)
    attended = attend(queries, kept, valid, AHD)
    return streams, attended


def solution(mesh):
    placed = (
        P("seq", "tp"), P("seq", None), P("seq", None), P("seq", "tp"), P("seq", "tp"),
        P("tp"), P("tp"), P("tp", None), P("seq", "tp"), P(), P(None, None, "tp"),
    )

    return jax.shard_map(
        on_device, mesh=mesh, in_specs=placed, out_specs=(P("seq", "tp"), P("seq", "tp")),
        check_vma=False,
    )
```

time: 425 us -> 226 us (0.53)
  waiting for transfers between devices: 220 us -> 76.6 us
  Pallas kernels: 0 us -> 84.9 us
  matrix products: 65 us -> 0 us
  local copies, waits for them, and re-layouts: 64.3 us -> 23.6 us
  blocking collectives: 30.9 us -> 0 us
  starting transfers between devices: 12 us -> 32 us
  between operations: 14.8 us -> 1.41 us
  other arithmetic: 15.9 us -> 4.75 us
    pallas_call x0 -> x12, Pallas kernels: none -> 84.9 us  [the longest x4 24.1 us: stream_and_project(): pl.pallas_call(kernel, grid=((parts - 1) * steps,), in_specs=[pl.BlockSpe...]
    all_gather x2 -> x0, waiting for transfers between devices: 61.4 us -> none  [the longest x1 35.1 us: prefix(): lax.all_gather(a.astype(kind), axis)]
    reduce_scatter x1 -> x0, waiting for transfers between devices: 55.1 us -> none  [on_device(): lax.psum_scatter(partial_value.astype(jnp.bfloat16), 'tp', scatter_dimens...]
    dot_general x7 -> x0, matrix products: 44.6 us -> none  [the longest x1 16.3 us: on_device(): jnp.einsum('htr,rhd->thd', weights, value_part, preferred_element_type=jn...]
    ppermute x4 -> x28, waiting for transfers between devices: 103 us -> 76.6 us  [the longest x5 29.7 us: swap(): return lax.ppermute(x, 'tp', [(0, 1), (1, 0)])]
    unnamed x1 -> x0, blocking collectives: 25.8 us -> none
    sub x1 -> x0, matrix products: 20.4 us -> none  [on_device(): raised = jnp.exp(masked - peak)]
    ppermute x4 -> x28, starting transfers between devices: 11.9 us -> 32 us  [the longest x7 18.8 us: shift(): return lax.ppermute(x, 'seq', [(i, i + by) for i in range(size - by)])]
  transfers between devices with their start and end apart: 7 -> 28, of which waited for: 7 -> 14; matrix products, arithmetic and copies ran while one was open for 7% -> 3% of each run, Pallas kernels for 0% -> 24%
where the time goes in v1:
time: 226 us; the launch traced here: 223 us
  Pallas kernels  84.9 us (38%)
  waiting for transfers between devices  76.6 us (34%)
  starting transfers between devices  32 us (14%)
  local copies, waits for them, and re-layouts  23.6 us (10%)
  other arithmetic  4.75 us (2%)
    ppermute x5, waiting for transfers between devices, swap(): return lax.ppermute(x, 'tp', [(0, 1), (1, 0)])  29.7 us
    ppermute x7, waiting for transfers between devices, shift(): return lax.ppermute(x, 'seq', [(i, i + by) for i in range(size - by)])  27.7 us
    pallas_call x4, Pallas kernels, stream_and_project(): pl.pallas_call(kernel, grid=((parts - 1) * steps,), in_specs=[pl.BlockSpe...  24.1 us
    unnamed x62, local copies, waits for them, and re-layouts  20 us
    ppermute x16, waiting for transfers between devices, flip(): return lax.ppermute(x, 'seq', [(i, i ^ bit) for i in range(size)])  19.2 us
    pallas_call x2, Pallas kernels, partial_outputs(): pl.pallas_call(kernel, grid=(channels // group,), in_specs=[pl.BlockSpec(...  19 us
    ppermute x7, starting transfers between devices, shift(): return lax.ppermute(x, 'seq', [(i, i + by) for i in range(size - by)])  18.8 us
    pallas_call x1, Pallas kernels, attend(): pl.pallas_call(kernel, grid=(groups,), in_specs=specs, out_specs=pl.Block...  18.8 us
  transfers between devices with their start and end apart: 28, of which 14 were waited for; matrix products, arithmetic and copies ran while one was open for 3% of the time, Pallas kernels for 24%

profile of v1, /device:TPU:8, one launch (start us, length us, event | category | flops | bytes accessed | tf_op | source)
XLA Modules:
  0.0 223.2 jit_solution(7944772075244194869)
XLA Ops:
  0.6 6.5 %write_states.1 = (bf16[1584,128]{1,0:T(8,128)(2,1)}, bf16[512,128]{1,0:T(8,128)(2,1)}, bf16[512,128]{1,0:T(8,128)(2,1)}, bf16[512,128]{1,0:T(8,128)(2,1)}, f32[512,128]{1,0:T(8,128)}, /*index=5*/f32[24,512]{1,0:T(8,128)}) custom-call(bf16[512,1536]{1,0:T(8,128)(2,1)} %x_ref.7, f32[24,512]{1,0:T(8,128)} %bitcast.45, f32[24,512]{1,0:T(8,128)} %bitcast.46, ...), custom_call_target="tpu_custom_call" | custom-call | flops 201326592 | bytes 1966080 | tf_op jit(solution)/shard_map/write_states/pallas_call | solution.py:304
  12.6 5.6 %collective-permute-done.1 = bf16[792,128]{1,0:T(8,128)(2,1)S(1)} collective-permute-done((bf16[792,128]{1,0:T(8,128)(2,1)S(1)}, bf16[792,128]{1,0:T(8,128)(2,1)S(1)}, u32[]{:S(2)}, u32[]{:S(2)}) %collective-permute-start.1) | collective-permute-done | bytes 202784 | tf_op jit(solution)/shard_map/ppermute | solution.py:504
  25.5 5.3 %collective-permute-done.3 = bf16[396,128]{1,0:T(8,128)(2,1)S(1)} collective-permute-done((bf16[396,128]{1,0:T(8,128)(2,1)S(1)}, bf16[396,128]{1,0:T(8,128)(2,1)S(1)}, u32[]{:S(2)}, u32[]{:S(2)}) %collective-permute-start.3) | collective-permute-done | bytes 101408 | tf_op jit(solution)/shard_map/ppermute | solution.py:509
  39.5 5.4 %local_outputs.3.refs_0_ = f32[512,1536]{1,0:T(8,128)} custom-call(bf16[512,1536]{1,0:T(8,128)(2,1)} %x_ref.7, bf16[512,128]{1,0:T(8,128)(2,1)} %get-tuple-element.23.p_ref, bf16[512,128]{1,0:T(8,128)(2,1)} %get-tuple-element.24.f_ref, f32[512,128]{1,0:T(8,128)} %get-tuple-element.25.t_ref, f32[6,4,512]{2,1,0:T(4,128)} %reshape.92.g_ref, ...), custom_call_target="tpu_custom_call" | custom-call | flops 402653184 | bytes 2359296 | tf_op jit(solution)/shard_map/local_outputs/pallas_call | solution.py:404
  44.9 4.5 %local_outputs.4.refs_0_ = f32[512,1536]{1,0:T(8,128)} custom-call(bf16[512,1536]{1,0:T(8,128)(2,1)} %x_ref.7, bf16[512,128]{1,0:T(8,128)(2,1)} %get-tuple-element.23.p_ref, bf16[512,128]{1,0:T(8,128)(2,1)} %get-tuple-element.24.f_ref, f32[512,128]{1,0:T(8,128)} %get-tuple-element.25.t_ref, ...), custom_call_target="tpu_custom_call", output_to_operand_aliasing={{}: (8, {})} | custom-call | flops 268435456 | bytes 1572864 | tf_op jit(solution)/shard_map/local_outputs/pallas_call | solution.py:404
  52.9 7.5 %partial_outputs.3.own_ref = bf16[128,3072]{1,0:T(8,128)(2,1)} custom-call(f32[512,1536]{1,0:T(8,128)} %local_outputs.5.y_ref, bf16[512,128]{1,0:T(8,128)(2,1)} %get-tuple-element.27.p_ref, bf16[512,128]{1,0:T(8,128)(2,1)} %c_ref.9, bf16[1536,128]{1,0:T(8,128)(2,1)S(1)} %fusion.1.s_ref, f32[1,1536]{1,0:T(1,128)S(1)} %broadcast_in_dim.13.g_ref, ...), custom_call_target="tpu_custom_call" | custom-call | flops 1207959552 | bytes 9437184 | tf_op jit(solution)/shard_map/partial_outputs/pallas_call | solution.py:478
  62.0 11.5 %partial_outputs.2 = (bf16[128,3072]{1,0:T(8,128)(2,1)}, bf16[128,3072]{1,0:T(8,128)(2,1)}, bf16[128,3072]{1,0:T(8,128)(2,1)}) custom-call(f32[512,1536]{1,0:T(8,128)} %local_outputs.5.y_ref, bf16[512,128]{1,0:T(8,128)(2,1)} %get-tuple-element.27.p_ref, bf16[512,128]{1,0:T(8,128)(2,1)} %c_ref.9, bf16[1536,128]{1,0:T(8,128)(2,1)S(1)} %fusion.1.s_ref, ...), custom_call_target="tpu_custom_call" | custom-call | flops 3623878656 | bytes 9437184 | tf_op jit(solution)/shard_map/partial_outputs/pallas_call | solution.py:478
  76.0 10.7 %collective-permute-done.11.got_ref = bf16[128,3072]{1,0:T(8,128)(2,1)S(1)} collective-permute-done((bf16[128,3072]{1,0:T(8,128)(2,1)}, bf16[128,3072]{1,0:T(8,128)(2,1)S(1)}, u32[]{:S(2)}, u32[]{:S(2)}) %collective-permute-start.11) | collective-permute-done | bytes 786464 | tf_op jit(solution)/shard_map/ppermute | solution.py:513
  87.6 5.0 %copy-done = bf16[3072,3,768]{2,0,1:T(8,128)(2,1)S(1)} copy-done((bf16[3072,3,768]{2,0,1:T(8,128)(2,1)S(1)}, bf16[3072,3,768]{2,0,1:T(8,128)(2,1)}, u32[]{:S(2)}) %copy-start) | copy-done | bytes 14155800
  93.7 5.8 %stream_and_project.4 = (bf16[512,1536]{1,0:T(8,128)(2,1)}, bf16[512,3072]{1,0:T(8,128)(2,1)S(1)}, bf16[128,1536]{1,0:T(8,128)(2,1)}) custom-call(s32[1]{0:T(128)} %bitcast.side_ref, bf16[128,3072]{1,0:T(8,128)(2,1)} %partial_outputs.3.own_ref, bf16[128,3072]{1,0:T(8,128)(2,1)S(1)} %copy-done.4, bf16[512,1536]{1,0:T(8,128)(2,1)} %res_ref.7, ...), custom_call_target="tpu_custom_call" | custom-call | flops 1207959552 | bytes 9437184 | tf_op jit(solution)/shard_map/stream_and_project/pallas_call | solution.py:152
  99.5 4.1 %collective-permute-done.10.got_ref = bf16[128,3072]{1,0:T(8,128)(2,1)} collective-permute-done((bf16[128,3072]{1,0:T(8,128)(2,1)}, bf16[128,3072]{1,0:T(8,128)(2,1)}, u32[]{:S(2)}, u32[]{:S(2)}) %collective-permute-start.10) | collective-permute-done | bytes 786464 | tf_op jit(solution)/shard_map/ppermute | solution.py:513
  103.7 5.0 %copy-done.1 = bf16[3072,3,768]{2,0,1:T(8,128)(2,1)S(1)} copy-done((bf16[3072,3,768]{2,0,1:T(8,128)(2,1)S(1)}, bf16[3072,3,768]{2,0,1:T(8,128)(2,1)}, u32[]{:S(2)}) %copy-start.1) | copy-done | bytes 14155800
  108.7 6.0 %stream_and_project.5 = (bf16[512,1536]{1,0:T(8,128)(2,1)}, bf16[512,3072]{1,0:T(8,128)(2,1)S(1)}, bf16[128,1536]{1,0:T(8,128)(2,1)}) custom-call(s32[1]{0:T(128)} %bitcast.side_ref, bf16[128,3072]{1,0:T(8,128)(2,1)} %get-tuple-element.31.own_ref, bf16[128,3072]{1,0:T(8,128)(2,1)} %collective-permute-done.10.got_ref, ...), custom_call_target="tpu_custom_call", output_to_operand_aliasing={{0}: (7, {}), {1}: (8, {})} | custom-call | flops 1207959552 | bytes 9437184 | tf_op jit(solution)/shard_map/stream_and_project/pallas_call | solution.py:152
  114.7 5.8 %collective-permute-done.9.got_ref = bf16[128,3072]{1,0:T(8,128)(2,1)} collective-permute-done((bf16[128,3072]{1,0:T(8,128)(2,1)}, bf16[128,3072]{1,0:T(8,128)(2,1)}, u32[]{:S(2)}, u32[]{:S(2)}) %collective-permute-start.9) | collective-permute-done | bytes 786464 | tf_op jit(solution)/shard_map/ppermute | solution.py:513
  120.5 6.0 %stream_and_project.6 = (bf16[512,1536]{1,0:T(8,128)(2,1)}, bf16[512,3072]{1,0:T(8,128)(2,1)S(1)}, bf16[128,1536]{1,0:T(8,128)(2,1)}) custom-call(s32[1]{0:T(128)} %bitcast.side_ref, bf16[128,3072]{1,0:T(8,128)(2,1)} %get-tuple-element.30.own_ref, bf16[128,3072]{1,0:T(8,128)(2,1)} %collective-permute-done.9.got_ref, ...), custom_call_target="tpu_custom_call", output_to_operand_aliasing={{0}: (7, {}), {1}: (8, {})} | custom-call | flops 1207959552 | bytes 9437184 | tf_op jit(solution)/shard_map/stream_and_project/pallas_call | solution.py:152
  126.5 9.1 %collective-permute-done.7.got_ref = bf16[128,3072]{1,0:T(8,128)(2,1)} collective-permute-done((bf16[128,3072]{1,0:T(8,128)(2,1)}, bf16[128,3072]{1,0:T(8,128)(2,1)}, u32[]{:S(2)}, u32[]{:S(2)}) %collective-permute-start.7) | collective-permute-done | bytes 786464 | tf_op jit(solution)/shard_map/ppermute | solution.py:513
  135.6 6.2 %stream_and_project.7 = (bf16[512,1536]{1,0:T(8,128)(2,1)}, bf16[512,3072]{1,0:T(8,128)(2,1)S(1)}, bf16[128,1536]{1,0:T(8,128)(2,1)}) custom-call(s32[1]{0:T(128)} %bitcast.side_ref, bf16[128,3072]{1,0:T(8,128)(2,1)} %get-tuple-element.29.own_ref, bf16[128,3072]{1,0:T(8,128)(2,1)} %collective-permute-done.7.got_ref, ...), custom_call_target="tpu_custom_call", output_to_operand_aliasing={{0}: (7, {}), {1}: (8, {})} | custom-call | flops 1207959552 | bytes 9437184 | tf_op jit(solution)/shard_map/stream_and_project/pallas_call | solution.py:152
  144.6 5.2 %collective-permute-start.14 = (bf16[128,1536]{1,0:T(8,128)(2,1)S(1)}, bf16[128,1536]{1,0:T(8,128)(2,1)S(1)}, u32[]{:S(2)}, u32[]{:S(2)}) collective-permute-start(bf16[128,1536]{1,0:T(8,128)(2,1)S(1)} %copy-done.8), channel_id=1, source_target_pairs={{0,8},{2,10},{4,12},{6,14},{8,16},{10,18},{12,20},{14,22},{16,24},... | collective-permute-start | bytes 1179656 | tf_op jit(solution)/shard_map/ppermute | solution.py:509
  157.7 6.6 %collective-permute-done.14.refs_4_.refs_5_ = bf16[128,1536]{1,0:T(8,128)(2,1)S(1)} collective-permute-done((bf16[128,1536]{1,0:T(8,128)(2,1)S(1)}, bf16[128,1536]{1,0:T(8,128)(2,1)S(1)}, u32[]{:S(2)}, u32[]{:S(2)}) %collective-permute-start.14) | collective-permute-done | bytes 393248 | tf_op jit(solution)/shard_map/ppermute | solution.py:509
  165.0 7.8 %collective-permute-done.13.refs_2_.refs_3_ = bf16[128,1536]{1,0:T(8,128)(2,1)S(1)} collective-permute-done((bf16[128,1536]{1,0:T(8,128)(2,1)S(1)}, bf16[128,1536]{1,0:T(8,128)(2,1)S(1)}, u32[]{:S(2)}, u32[]{:S(2)}) %collective-permute-start.13) | collective-permute-done | bytes 393248 | tf_op jit(solution)/shard_map/ppermute | solution.py:509
  172.8 5.7 %collective-permute-done.12.refs_0_.refs_1_ = bf16[128,1536]{1,0:T(8,128)(2,1)S(1)} collective-permute-done((bf16[128,1536]{1,0:T(8,128)(2,1)S(1)}, bf16[128,1536]{1,0:T(8,128)(2,1)S(1)}, u32[]{:S(2)}, u32[]{:S(2)}) %collective-permute-start.12) | collective-permute-done | bytes 393248 | tf_op jit(solution)/shard_map/ppermute | solution.py:509
  183.5 6.8 %collective-permute-done.21.refs_18_.refs_19_ = bf16[128,1536]{1,0:T(8,128)(2,1)} collective-permute-done((bf16[128,1536]{1,0:T(8,128)(2,1)S(1)}, bf16[128,1536]{1,0:T(8,128)(2,1)}, u32[]{:S(2)}, u32[]{:S(2)}) %collective-permute-start.21) | collective-permute-done | bytes 393248 | tf_op jit(solution)/shard_map/ppermute | solution.py:504
  195.7 5.0 %copy-done.2 = bf16[3072,3,768]{2,0,1:T(8,128)(2,1)S(1)} copy-done((bf16[3072,3,768]{2,0,1:T(8,128)(2,1)S(1)}, bf16[3072,3,768]{2,0,1:T(8,128)(2,1)}, u32[]{:S(2)}) %copy-start.2) | copy-done | bytes 14155800
  204.3 18.8 %attend.1 = bf16[512,768]{1,0:T(8,128)(2,1)} custom-call(s32[4]{0:T(128)S(1)} %compare_convert_fusion.valid_ref, bf16[512,768]{1,0:T(8,128)(2,1)S(1)} %project_queries.1.q_ref, bf16[128,1536]{1,0:T(8,128)(2,1)S(1)} %copy-done.18, bf16[128,1536]{1,0:T(8,128)(2,1)S(1)} %copy-done.18, bf16[128,1536]{1,0:T(8,128)(2,1)S(1)} %copy-done.16, ...), custom_call_target="tpu_custom_call" | custom-call | flops 4026531840 | bytes 9437184 | tf_op jit(solution)/shard_map/attend/pallas_call | solution.py:99
  (145 shorter events, 55.7 us)
Async XLA Ops:
  19.1 11.8 %collective-permute-start.2 = (bf16[396,128]{1,0:T(8,128)(2,1)S(1)}, bf16[396,128]{1,0:T(8,128)(2,1)S(1)}, u32[]{:S(2)}, u32[]{:S(2)}) collective-permute-start(bf16[396,128]{1,0:T(8,128)(2,1)S(1)} %pad_maximum_fusion.1), channel_id=1, source_target_pairs={{0,8},{2,10},{4,12},{6,14},{8,16},{10,18},{12,20},{14,22},{16,24},... | collective-permute-start | bytes 304136 | tf_op jit(solution)/shard_map/ppermute | solution.py:509
  22.6 8.3 %collective-permute-start.3 = (bf16[396,128]{1,0:T(8,128)(2,1)S(1)}, bf16[396,128]{1,0:T(8,128)(2,1)S(1)}, u32[]{:S(2)}, u32[]{:S(2)}) collective-permute-start(bf16[396,128]{1,0:T(8,128)(2,1)S(1)} %pad_maximum_fusion.1), channel_id=1, source_target_pairs={{0,16},{2,18},{4,20},{6,22},{8,24},{10,26},{12,28},{14,30},{1,17},... | collective-permute-start | bytes 304136 | tf_op jit(solution)/shard_map/ppermute | solution.py:509
  32.6 43.4 %collective-permute-start.8 = (bf16[512,1536]{1,0:T(8,128)(2,1)S(1)}, bf16[512,1536]{1,0:T(8,128)(2,1)}, u32[]{:S(2)}, u32[]{:S(2)}) collective-permute-start(bf16[512,1536]{1,0:T(8,128)(2,1)S(1)} %copy-done.25), channel_id=1, source_target_pairs={{0,1},{1,0},{2,3},{3,2},{4,5},{5,4},{6,7},{7,6},{8,9},{9,8},{10,11... | collective-permute-start | bytes 4718600 | tf_op jit(solution)/shard_map/ppermute | solution.py:513
  35.8 16.8 %collective-permute-start.6 = (bf16[12,64,128]{2,1,0:T(8,128)(2,1)S(1)}, bf16[12,64,128]{2,1,0:T(8,128)(2,1)S(1)}, u32[]{:S(2)}, u32[]{:S(2)}) collective-permute-start(bf16[12,64,128]{2,1,0:T(8,128)(2,1)S(1)} %fusion.3), channel_id=1, source_target_pairs={{0,2},{2,0},{4,6},{6,4},{8,10},{10,8},{12,14},{14,12},{16,18},{18,... | collective-permute-start | bytes 589832 | tf_op jit(solution)/shard_map/ppermute | solution.py:504
  60.4 26.3 %collective-permute-start.11 = (bf16[128,3072]{1,0:T(8,128)(2,1)}, bf16[128,3072]{1,0:T(8,128)(2,1)S(1)}, u32[]{:S(2)}, u32[]{:S(2)}) collective-permute-start(bf16[128,3072]{1,0:T(8,128)(2,1)} %partial_outputs.3.own_ref), channel_id=1, source_target_pairs={{0,1},{1,0},{2,3},{3,2},{4,5},{5,4},{6,7},{7,6},{8,9},{9,8},{10,11... | collective-permute-start | bytes 2359304 | tf_op jit(solution)/shard_map/ppermute | solution.py:513
  73.5 30.2 %collective-permute-start.10 = (bf16[128,3072]{1,0:T(8,128)(2,1)}, bf16[128,3072]{1,0:T(8,128)(2,1)}, u32[]{:S(2)}, u32[]{:S(2)}) collective-permute-start(bf16[128,3072]{1,0:T(8,128)(2,1)} %get-tuple-element.31.own_ref), channel_id=1, source_target_pairs={{0,1},{1,0},{2,3},{3,2},{4,5},{5,4},{6,7},{7,6},{8,9},{9,8},{10,11... | collective-permute-start | bytes 2359304 | tf_op jit(solution)/shard_map/ppermute | solution.py:513
  74.0 46.5 %collective-permute-start.9 = (bf16[128,3072]{1,0:T(8,128)(2,1)}, bf16[128,3072]{1,0:T(8,128)(2,1)}, u32[]{:S(2)}, u32[]{:S(2)}) collective-permute-start(bf16[128,3072]{1,0:T(8,128)(2,1)} %get-tuple-element.30.own_ref), channel_id=1, source_target_pairs={{0,1},{1,0},{2,3},{3,2},{4,5},{5,4},{6,7},{7,6},{8,9},{9,8},{10,11... | collective-permute-start | bytes 2359304 | tf_op jit(solution)/shard_map/ppermute | solution.py:513
  75.5 60.1 %collective-permute-start.7 = (bf16[128,3072]{1,0:T(8,128)(2,1)}, bf16[128,3072]{1,0:T(8,128)(2,1)}, u32[]{:S(2)}, u32[]{:S(2)}) collective-permute-start(bf16[128,3072]{1,0:T(8,128)(2,1)} %get-tuple-element.29.own_ref), channel_id=1, source_target_pairs={{0,1},{1,0},{2,3},{3,2},{4,5},{5,4},{6,7},{7,6},{8,9},{9,8},{10,11... | collective-permute-start | bytes 2359304 | tf_op jit(solution)/shard_map/ppermute | solution.py:513
  141.8 14.1 %collective-permute-start.15 = (bf16[128,1536]{1,0:T(8,128)(2,1)}, bf16[128,1536]{1,0:T(8,128)(2,1)S(1)}, u32[]{:S(2)}, u32[]{:S(2)}) collective-permute-start(bf16[128,1536]{1,0:T(8,128)(2,1)} %get-tuple-element.43.refs_38_.refs_39_), channel_id=1, source_target_pairs={{0,8},{2,10},{4,12},{6,14},{8,16},{10,18},{12,20},{14,22},{16,24},... | collective-permute-start | bytes 1179656 | tf_op jit(solution)/shard_map/ppermute | solution.py:509
  144.6 19.8 %collective-permute-start.14 = (bf16[128,1536]{1,0:T(8,128)(2,1)S(1)}, bf16[128,1536]{1,0:T(8,128)(2,1)S(1)}, u32[]{:S(2)}, u32[]{:S(2)}) collective-permute-start(bf16[128,1536]{1,0:T(8,128)(2,1)S(1)} %copy-done.8), channel_id=1, source_target_pairs={{0,8},{2,10},{4,12},{6,14},{8,16},{10,18},{12,20},{14,22},{16,24},... | collective-permute-start | bytes 1179656 | tf_op jit(solution)/shard_map/ppermute | solution.py:509
  149.8 23.0 %collective-permute-start.13 = (bf16[128,1536]{1,0:T(8,128)(2,1)S(1)}, bf16[128,1536]{1,0:T(8,128)(2,1)S(1)}, u32[]{:S(2)}, u32[]{:S(2)}) collective-permute-start(bf16[128,1536]{1,0:T(8,128)(2,1)S(1)} %copy-done.6), channel_id=1, source_target_pairs={{0,8},{2,10},{4,12},{6,14},{8,16},{10,18},{12,20},{14,22},{16,24},... | collective-permute-start | bytes 1179656 | tf_op jit(solution)/shard_map/ppermute | solution.py:509
  151.7 26.9 %collective-permute-start.12 = (bf16[128,1536]{1,0:T(8,128)(2,1)S(1)}, bf16[128,1536]{1,0:T(8,128)(2,1)S(1)}, u32[]{:S(2)}, u32[]{:S(2)}) collective-permute-start(bf16[128,1536]{1,0:T(8,128)(2,1)S(1)} %copy-done.5), channel_id=1, source_target_pairs={{0,8},{2,10},{4,12},{6,14},{8,16},{10,18},{12,20},{14,22},{16,24},... | collective-permute-start | bytes 1179656 | tf_op jit(solution)/shard_map/ppermute | solution.py:509
  157.1 22.8 %collective-permute-start.23 = (bf16[128,1536]{1,0:T(8,128)(2,1)S(1)}, bf16[128,1536]{1,0:T(8,128)(2,1)}, u32[]{:S(2)}, u32[]{:S(2)}) collective-permute-start(bf16[128,1536]{1,0:T(8,128)(2,1)S(1)} %get-tuple-element.60), channel_id=1, source_target_pairs={{0,4},{2,6},{4,0},{6,2},{8,12},{10,14},{12,8},{14,10},{16,20},{18,... | collective-permute-start | bytes 1179656 | tf_op jit(solution)/shard_map/ppermute | solution.py:504
  157.7 22.3 %collective-permute-start.19 = (bf16[128,1536]{1,0:T(8,128)(2,1)S(1)}, bf16[128,1536]{1,0:T(8,128)(2,1)S(1)}, u32[]{:S(2)}, u32[]{:S(2)}) collective-permute-start(bf16[128,1536]{1,0:T(8,128)(2,1)S(1)} %get-tuple-element.61), channel_id=1, source_target_pairs={{0,2},{2,0},{4,6},{6,4},{8,10},{10,8},{12,14},{14,12},{16,18},{18,... | collective-permute-start | bytes 1179656 | tf_op jit(solution)/shard_map/ppermute | solution.py:504
  164.4 17.9 %collective-permute-start.22 = (bf16[128,1536]{1,0:T(8,128)(2,1)S(1)}, bf16[128,1536]{1,0:T(8,128)(2,1)}, u32[]{:S(2)}, u32[]{:S(2)}) collective-permute-start(bf16[128,1536]{1,0:T(8,128)(2,1)S(1)} %get-tuple-element.62), channel_id=1, source_target_pairs={{0,4},{2,6},{4,0},{6,2},{8,12},{10,14},{12,8},{14,10},{16,20},{18,... | collective-permute-start | bytes 1179656 | tf_op jit(solution)/shard_map/ppermute | solution.py:504
  172.8 9.7 %collective-permute-start.18 = (bf16[128,1536]{1,0:T(8,128)(2,1)S(1)}, bf16[128,1536]{1,0:T(8,128)(2,1)S(1)}, u32[]{:S(2)}, u32[]{:S(2)}) collective-permute-start(bf16[128,1536]{1,0:T(8,128)(2,1)S(1)} %get-tuple-element.63), channel_id=1, source_target_pairs={{0,2},{2,0},{4,6},{6,4},{8,10},{10,8},{12,14},{14,12},{16,18},{18,... | collective-permute-start | bytes 1179656 | tf_op jit(solution)/shard_map/ppermute | solution.py:504
  178.6 11.8 %collective-permute-start.21 = (bf16[128,1536]{1,0:T(8,128)(2,1)S(1)}, bf16[128,1536]{1,0:T(8,128)(2,1)}, u32[]{:S(2)}, u32[]{:S(2)}) collective-permute-start(bf16[128,1536]{1,0:T(8,128)(2,1)S(1)} %get-tuple-element.64), channel_id=1, source_target_pairs={{0,4},{2,6},{4,0},{6,2},{8,12},{10,14},{12,8},{14,10},{16,20},{18,... | collective-permute-start | bytes 1179656 | tf_op jit(solution)/shard_map/ppermute | solution.py:504
  180.0 10.4 %collective-permute-start.17 = (bf16[128,1536]{1,0:T(8,128)(2,1)S(1)}, bf16[128,1536]{1,0:T(8,128)(2,1)S(1)}, u32[]{:S(2)}, u32[]{:S(2)}) collective-permute-start(bf16[128,1536]{1,0:T(8,128)(2,1)S(1)} %get-tuple-element.65), channel_id=1, source_target_pairs={{0,2},{2,0},{4,6},{6,4},{8,10},{10,8},{12,14},{14,12},{16,18},{18,... | collective-permute-start | bytes 1179656 | tf_op jit(solution)/shard_map/ppermute | solution.py:504
  180.8 14.8 %collective-permute-start.20 = (bf16[128,1536]{1,0:T(8,128)(2,1)S(1)}, bf16[128,1536]{1,0:T(8,128)(2,1)}, u32[]{:S(2)}, u32[]{:S(2)}) collective-permute-start(bf16[128,1536]{1,0:T(8,128)(2,1)S(1)} %get-tuple-element.66), channel_id=1, source_target_pairs={{0,4},{2,6},{4,0},{6,2},{8,12},{10,14},{12,8},{14,10},{16,20},{18,... | collective-permute-start | bytes 1179656 | tf_op jit(solution)/shard_map/ppermute | solution.py:504
  182.3 21.8 %collective-permute-start.16 = (bf16[128,1536]{1,0:T(8,128)(2,1)}, bf16[128,1536]{1,0:T(8,128)(2,1)}, u32[]{:S(2)}, u32[]{:S(2)}) collective-permute-start(bf16[128,1536]{1,0:T(8,128)(2,1)} %get-tuple-element.67), channel_id=1, source_target_pairs={{0,2},{2,0},{4,6},{6,4},{8,10},{10,8},{12,14},{14,12},{16,18},{18,... | collective-permute-start | bytes 1179656 | tf_op jit(solution)/shard_map/ppermute | solution.py:504
  183.2 20.9 %collective-permute-start.27 = (bf16[128,1536]{1,0:T(8,128)(2,1)}, bf16[128,1536]{1,0:T(8,128)(2,1)}, u32[]{:S(2)}, u32[]{:S(2)}) collective-permute-start(bf16[128,1536]{1,0:T(8,128)(2,1)} %collective-permute-done.23.refs_22_.refs_23_), channel_id=1, source_target_pairs={{0,2},{2,0},{4,6},{6,4},{8,10},{10,8},{12,14},{14,12},{16,18},{18,... | collective-permute-start | bytes 1179656 | tf_op jit(solution)/shard_map/ppermute | solution.py:504
  190.4 13.8 %collective-permute-start.26 = (bf16[128,1536]{1,0:T(8,128)(2,1)}, bf16[128,1536]{1,0:T(8,128)(2,1)}, u32[]{:S(2)}, u32[]{:S(2)}) collective-permute-start(bf16[128,1536]{1,0:T(8,128)(2,1)} %collective-permute-done.22.refs_20_.refs_21_), channel_id=1, source_target_pairs={{0,2},{2,0},{4,6},{6,4},{8,10},{10,8},{12,14},{14,12},{16,18},{18,... | collective-permute-start | bytes 1179656 | tf_op jit(solution)/shard_map/ppermute | solution.py:504
  191.1 13.0 %collective-permute-start.25 = (bf16[128,1536]{1,0:T(8,128)(2,1)}, bf16[128,1536]{1,0:T(8,128)(2,1)}, u32[]{:S(2)}, u32[]{:S(2)}) collective-permute-start(bf16[128,1536]{1,0:T(8,128)(2,1)} %collective-permute-done.21.refs_18_.refs_19_), channel_id=1, source_target_pairs={{0,2},{2,0},{4,6},{6,4},{8,10},{10,8},{12,14},{14,12},{16,18},{18,... | collective-permute-start | bytes 1179656 | tf_op jit(solution)/shard_map/ppermute | solution.py:504
  195.6 8.6 %collective-permute-start.24 = (bf16[128,1536]{1,0:T(8,128)(2,1)}, bf16[128,1536]{1,0:T(8,128)(2,1)}, u32[]{:S(2)}, u32[]{:S(2)}) collective-permute-start(bf16[128,1536]{1,0:T(8,128)(2,1)} %collective-permute-done.20.refs_16_.refs_17_), channel_id=1, source_target_pairs={{0,2},{2,0},{4,6},{6,4},{8,10},{10,8},{12,14},{14,12},{16,18},{18,... | collective-permute-start | bytes 1179656 | tf_op jit(solution)/shard_map/ppermute | solution.py:504
  (35 other events, 207.6 us)
